TPU v7x, 256 devices: a whole 4x4x8 slice. The times are simulated.
256 devices in a mesh: chain: 8 (over z), rows: 32 (over y, x, core).
Axes of the slice: x: 4, y: 4, z: 8, core: 2. Of those that a mesh axis runs over, the one named last changes fastest.
Arguments:
- right_side: bfloat16 [16384, 768], P(('chain', 'rows')), may hold values from -6 to 6
- entering: float32 [16384, 256], P(('chain', 'rows')), may hold values from -6 to 6
- first_updates: float32 [2048, 512], P('rows'), may hold values from -6 to 6
- diag_inverse: bfloat16 [8, 2048, 2048], P('chain', 'rows'), may hold values from -2 to 2, as said below
- tile_blocks: bfloat16 [8, 32, 128, 2048], P('chain', 'rows'), may hold values from -0.09375 to 0.09375
- target_row_blocks: int32 [8, 32], P('chain', 'rows'), may hold values from 0 to 15
- tile_usage_order: int32 [8, 32], P('chain'), may hold values from 0 to 31, each once within a row
- live_tile_count: int32 [8], P('chain'), may hold values from 8 to 32
Outputs:
- solution: float32 [16384, 768], P(('chain', 'rows'))
- updates: float32 [16384, 768], P(('chain', 'rows'))
Inputs may be any that keep to these rules, and one draw needn't show every extreme that they name: `diag_inverse`: lower triangular. `tile_usage_order`: each row names each of the 32 slots once; the first live_tile_count[s] entries name the live slots of supernode s.
All inputs are finite; a program needn't handle non-finite values.
Results may differ from a plain program's by a relative error of at most 0.013.
Values may be sent and summed in bfloat16 or wider, within the bound.
A program may use at most 64 MiB of HBM per device.

v0:
```python
import jax
import jax.numpy as jnp
from jax import lax
from jax.sharding import PartitionSpec as P

PW = 256


def sent_to_all(array, axis):
    devices = lax.axis_size(axis)
    return lax.all_to_all(
        jnp.broadcast_to(array[None], (devices, *array.shape)), axis, 0, 0, tiled=True
    )


def laid_out(parts, dim):
    parts = jnp.moveaxis(parts, 0, dim)
    shape = parts.shape
    return parts.reshape(*shape[:dim], shape[dim] * shape[dim + 1], *shape[dim + 2 :])


def gathered_copies(array, axis, dim):
    parts = sent_to_all(array, axis)
    return laid_out(parts, dim)


def cut_along(array, dim, devices):
    before, after = (array.shape[:dim], array.shape[dim + 1 :])
    return jnp.moveaxis(array.reshape(*before, devices, -1, *after), dim, 0)


def sum_at_owner(array, axis, dim):
    devices = lax.axis_size(axis)
    parts = lax.all_to_all(cut_along(array, dim, devices), axis, 0, 0, tiled=True)
    return jnp.sum(parts.astype(jnp.float32), axis=0)


def shifted(block, axis, distance):
    devices = range(lax.axis_size(axis))
    route = [(i - distance, i) for i in devices if i - distance in devices]
    return lax.ppermute(block, axis, route)


def active_slot_list(tile_usage_order, live_tile_count, leading_part, slot_entries):
    every_slot = tile_usage_order.shape[1]
    positions = lax.broadcasted_iota(jnp.int32, (1, every_slot), 1)
    counted = positions < live_tile_count[0]
    wanted = leading_part + lax.broadcasted_iota(jnp.int32, (slot_entries, 1), 0)
    matches = jnp.logical_and(tile_usage_order[0][None, :] == wanted, counted)
    return jnp.sum(matches.astype(jnp.float32), axis=1)


def body(
    right_side,
    entering,
    first_updates,
    diag_inverse,
    tile_blocks,
    target_row_blocks,
    tile_usage_order,
    live_tile_count,
):
    slot_entries = tile_blocks.shape[1]
    tile_height = tile_blocks.shape[2]
    separator = tile_blocks.shape[3]
    ticks_total = right_side.shape[1] // PW
    row_blocks = separator // tile_height
    is_first = (lax.axis_index("chain") == 0).astype(jnp.float32)
    leading_part = lax.axis_index("rows") * slot_entries
    slot_alive_flags = active_slot_list(
        tile_usage_order, live_tile_count, leading_part, slot_entries
    )
    block_grid = lax.broadcasted_iota(jnp.int32, (row_blocks, slot_entries), 0)
    tile_placement_map = (block_grid == target_row_blocks[0][None, :]).astype(
        jnp.float32
    ) * slot_alive_flags[None, :]
    inverse_rows = diag_inverse[0]
    own_tiles = tile_blocks[0]
    solved_list = []
    passed_list = []
    incoming = entering
    for tick in range(ticks_total):
        head_rows = (
            right_side[:, tick * PW : (tick + 1) * PW].astype(jnp.float32) - incoming
        ).astype(jnp.bfloat16)
        portion = gathered_copies(head_rows, "rows", 0)
        solved = jnp.dot(inverse_rows, portion, preferred_element_type=jnp.float32)
        products = jnp.einsum("mtw,wp->mtp", own_tiles, portion, preferred_element_type=jnp.float32)
        one_solved = solved
        partial_value = jnp.einsum(
            "bm,mtp->btp", tile_placement_map, products, precision=lax.Precision.HIGHEST
        ).reshape(separator, PW)
        passed = sum_at_owner(partial_value.astype(jnp.bfloat16), "rows", 0)
        solved, passed = (one_solved, passed)
        solved_list.append(solved)
        passed_list.append(passed)
        if tick + 1 < ticks_total:
            moved = shifted(passed.astype(jnp.bfloat16), "chain", 1).astype(passed.dtype)
            incoming = moved + is_first * first_updates[:, tick * PW : (tick + 1) * PW]
    return (jnp.concatenate(solved_list, axis=1), jnp.concatenate(passed_list, axis=1))


def solution(mesh):
    placed = (
        P(("chain", "rows"), None),
        P(("chain", "rows"), None),
        P("rows", None),
        P("chain", "rows", None),
        P("chain", "rows", None, None),
        P("chain", "rows"),
        P("chain", None),
        P("chain"),
    )
    return jax.shard_map(
        body,
        mesh=mesh,
        in_specs=placed,
        out_specs=(P(("chain", "rows"), None), P(("chain", "rows"), None)),
        check_vma=False,
    )
```

profile of v0, /device:TPU:129, one launch (start us, length us, event | category | flops | bytes accessed | tf_op | source)
XLA Modules:
  0.0 153.1 jit_solution(9021840162002058445)
XLA Ops:
  0.6 0.9 subtract_convert_fusion.2
  1.6 1.1 broadcast_in_dim.6
  2.7 7.9 %all-to-all-start = ((bf16[32,64,256]{2,1,0:T(8,128)(2,1)}), bf16[32,64,256]{2,1,0:T(8,128)(2,1)S(1)}, u32[]{:S(2)}, u32[]{:S(2)}) async-start(bf16[32,64,256]{2,1,0:T(8,128)(2,1)} %broadcast_in_dim.6), calls=%async_computation | async-start | bytes 2097152 | tf_op jit(solution)/shard_map/all_to_all | solution.py:11
  11.9 0.6 fusion.6
  12.5 0.6 compare_select_fusion
  13.1 14.5 %all-to-all-done = bf16[32,64,256]{2,1,0:T(8,128)(2,1)S(1)} async-done(((bf16[32,64,256]{2,1,0:T(8,128)(2,1)}), bf16[32,64,256]{2,1,0:T(8,128)(2,1)S(1)}, u32[]{:S(2)}, u32[]{:S(2)}) %all-to-all-start) | async-done | bytes 1048608 | tf_op jit(solution)/shard_map/all_to_all | solution.py:11
  27.6 0.5 convolution_bitcast_fusion.2
  28.2 0.3 multiply_convert_fusion.2
  28.5 20.7 %all_to_all.30 = bf16[32,64,256]{2,1,0:T(8,128)(2,1)S(1)} all-to-all(bf16[32,64,256]{2,1,0:T(8,128)(2,1)S(1)} %bitcast.49), channel_id=1, replica_groups=mesh['chain'=8,'rows'=32] {'rows'}, dimensions={0} | all-to-all | bytes 2097152 | tf_op jit(solution)/shard_map/all_to_all | solution.py:34
  49.1 0.2 convert_reduce_fusion.2
  49.3 2.6 %collective-permute-start = (bf16[64,256]{1,0:T(8,128)(2,1)S(1)}, bf16[64,256]{1,0:T(8,128)(2,1)S(1)}, u32[]{:S(2)}, u32[]{:S(2)}) collective-permute-start(bf16[64,256]{1,0:T(8,128)(2,1)S(1)} %convert_element_type.74), channel_id=1, source_target_pairs={{0,32},{32,64},{64,96},{96,128},{128,160},{160,192},{192,224},{1,3... | collective-permute-start | bytes 98312 | tf_op jit(solution)/shard_map/ppermute | solution.py:41
  52.0 3.2 %collective-permute-done = bf16[64,256]{1,0:T(8,128)(2,1)S(1)} collective-permute-done((bf16[64,256]{1,0:T(8,128)(2,1)S(1)}, bf16[64,256]{1,0:T(8,128)(2,1)S(1)}, u32[]{:S(2)}, u32[]{:S(2)}) %collective-permute-start) | collective-permute-done | bytes 32800 | tf_op jit(solution)/shard_map/ppermute | solution.py:41
  55.3 21.5 %all_to_all.31 = bf16[32,64,256]{2,1,0:T(8,128)(2,1)S(1)} all-to-all(bf16[32,64,256]{2,1,0:T(8,128)(2,1)S(1)} %broadcast_in_dim.7), channel_id=1, replica_groups=mesh['chain'=8,'rows'=32] {'rows'}, dimensions={0} | all-to-all | bytes 2097152 | tf_op jit(solution)/shard_map/all_to_all | solution.py:11
  76.9 0.5 convolution_bitcast_fusion.1
  77.4 0.3 multiply_convert_fusion.1
  77.7 20.7 %all_to_all.32 = bf16[32,64,256]{2,1,0:T(8,128)(2,1)S(1)} all-to-all(bf16[32,64,256]{2,1,0:T(8,128)(2,1)S(1)} %bitcast.50), channel_id=1, replica_groups=mesh['chain'=8,'rows'=32] {'rows'}, dimensions={0} | all-to-all | bytes 2097152 | tf_op jit(solution)/shard_map/all_to_all | solution.py:34
  98.4 0.2 convert_reduce_fusion.1
  98.6 1.9 %collective-permute-start.1 = (bf16[64,256]{1,0:T(8,128)(2,1)S(1)}, bf16[64,256]{1,0:T(8,128)(2,1)S(1)}, u32[]{:S(2)}, u32[]{:S(2)}) collective-permute-start(bf16[64,256]{1,0:T(8,128)(2,1)S(1)} %convert_element_type.82), channel_id=1, source_target_pairs={{0,32},{32,64},{64,96},{96,128},{128,160},{160,192},{192,224},{1,3... | collective-permute-start | bytes 98312 | tf_op jit(solution)/shard_map/ppermute | solution.py:41
  100.5 3.9 %collective-permute-done.1 = bf16[64,256]{1,0:T(8,128)(2,1)S(1)} collective-permute-done((bf16[64,256]{1,0:T(8,128)(2,1)S(1)}, bf16[64,256]{1,0:T(8,128)(2,1)S(1)}, u32[]{:S(2)}, u32[]{:S(2)}) %collective-permute-start.1) | collective-permute-done | bytes 32800 | tf_op jit(solution)/shard_map/ppermute | solution.py:41
  104.6 21.5 %all_to_all.33 = bf16[32,64,256]{2,1,0:T(8,128)(2,1)S(1)} all-to-all(bf16[32,64,256]{2,1,0:T(8,128)(2,1)S(1)} %broadcast_in_dim.8), channel_id=1, replica_groups=mesh['chain'=8,'rows'=32] {'rows'}, dimensions={0} | all-to-all | bytes 2097152 | tf_op jit(solution)/shard_map/all_to_all | solution.py:11
  126.1 1.0 copy-done.1
  127.1 0.5 convolution_bitcast_fusion
  127.7 1.3 multiply_convert_fusion
  129.0 4.8 %all-to-all-start.5 = ((bf16[32,64,256]{2,1,0:T(8,128)(2,1)}), bf16[32,64,256]{2,1,0:T(8,128)(2,1)}, u32[]{:S(2)}, u32[]{:S(2)}) async-start(bf16[32,64,256]{2,1,0:T(8,128)(2,1)} %bitcast.48), calls=%async_computation.5 | async-start | bytes 2097152 | tf_op jit(solution)/shard_map/all_to_all | solution.py:34
  133.8 0.3 convolution_bitcast_fusion.5
  134.1 0.3 convolution_bitcast_fusion.4
  134.4 0.6 copy-done.2
  135.0 0.3 convolution_bitcast_fusion.3
  135.3 0.7 pad_maximum_fusion
  136.0 15.0 %all-to-all-done.5 = bf16[32,64,256]{2,1,0:T(8,128)(2,1)} async-done(((bf16[32,64,256]{2,1,0:T(8,128)(2,1)}), bf16[32,64,256]{2,1,0:T(8,128)(2,1)}, u32[]{:S(2)}, u32[]{:S(2)}) %all-to-all-start.5) | async-done | bytes 1048608 | tf_op jit(solution)/shard_map/all_to_all | solution.py:34
  151.0 1.4 convert_reduce_fusion
  152.4 0.7 pad_maximum_fusion.1
  (21 shorter events, 0.6 us)
Async XLA Ops:
  0.6 27.0 %copy-start = (bf16[1,1,128,2048]{3,2,1,0:T(8,128)(2,1)S(1)}, bf16[1,1,128,2048]{3,2,1,0:T(8,128)(2,1)}, u32[]{:S(2)}) copy-start(bf16[1,1,128,2048]{3,2,1,0:T(8,128)(2,1)} %param.12) | copy-start | bytes 1572868
  2.7 9.2 %copy-start.6 = (s32[1,32]{1,0:T(1,128)S(1)}, s32[1,32]{1,0:T(1,128)}, u32[]{:S(2)}) copy-start(s32[1,32]{1,0:T(1,128)} %param.14) | copy-start | bytes 388
  2.7 24.9 %all-to-all-start = ((bf16[32,64,256]{2,1,0:T(8,128)(2,1)}), bf16[32,64,256]{2,1,0:T(8,128)(2,1)S(1)}, u32[]{:S(2)}, u32[]{:S(2)}) async-start(bf16[32,64,256]{2,1,0:T(8,128)(2,1)} %broadcast_in_dim.6), calls=%async_computation | async-start | bytes 2097152 | tf_op jit(solution)/shard_map/all_to_all | solution.py:11
  49.1 6.0 %copy-start.4 = (f32[64,512]{1,0:T(8,128)S(1)}, f32[64,512]{1,0:T(8,128)}, u32[]{:S(2)}) copy-start(f32[64,512]{1,0:T(8,128)} %param.10) | copy-start | bytes 393220
  49.1 6.0 %copy-start.5 = (bf16[64,768]{1,0:T(8,128)(2,1)S(1)}, bf16[64,768]{1,0:T(8,128)(2,1)}, u32[]{:S(2)}) copy-start(bf16[64,768]{1,0:T(8,128)(2,1)} %param.8) | copy-start | bytes 294916
  49.3 5.9 %collective-permute-start = (bf16[64,256]{1,0:T(8,128)(2,1)S(1)}, bf16[64,256]{1,0:T(8,128)(2,1)S(1)}, u32[]{:S(2)}, u32[]{:S(2)}) collective-permute-start(bf16[64,256]{1,0:T(8,128)(2,1)S(1)} %convert_element_type.74), channel_id=1, source_target_pairs={{0,32},{32,64},{64,96},{96,128},{128,160},{160,192},{192,224},{1,3... | collective-permute-start | bytes 98312 | tf_op jit(solution)/shard_map/ppermute | solution.py:41
  98.6 5.9 %collective-permute-start.1 = (bf16[64,256]{1,0:T(8,128)(2,1)S(1)}, bf16[64,256]{1,0:T(8,128)(2,1)S(1)}, u32[]{:S(2)}, u32[]{:S(2)}) collective-permute-start(bf16[64,256]{1,0:T(8,128)(2,1)S(1)} %convert_element_type.82), channel_id=1, source_target_pairs={{0,32},{32,64},{64,96},{96,128},{128,160},{160,192},{192,224},{1,3... | collective-permute-start | bytes 98312 | tf_op jit(solution)/shard_map/ppermute | solution.py:41
  126.1 1.0 copy-start.1
  129.0 4.8 %copy-start.3 = (bf16[1,64,2048]{2,1,0:T(8,128)(2,1)S(1)}, bf16[1,64,2048]{2,1,0:T(8,128)(2,1)}, u32[]{:S(2)}) copy-start(bf16[1,64,2048]{2,1,0:T(8,128)(2,1)} %param.11) | copy-start | bytes 786436
  129.0 22.0 %all-to-all-start.5 = ((bf16[32,64,256]{2,1,0:T(8,128)(2,1)}), bf16[32,64,256]{2,1,0:T(8,128)(2,1)}, u32[]{:S(2)}, u32[]{:S(2)}) async-start(bf16[32,64,256]{2,1,0:T(8,128)(2,1)} %bitcast.48), calls=%async_computation.5 | async-start | bytes 2097152 | tf_op jit(solution)/shard_map/all_to_all | solution.py:34
  133.8 1.2 copy-start.2
where the time goes:
time: 154 us; the launch traced here: 153 us
  blocking collectives  84.4 us (55%)
  waiting for transfers between devices  36.6 us (24%)
  starting transfers between devices  17.2 us (11%)
  other arithmetic  7.13 us (5%)
  local copies, waits for them, and re-layouts  3.27 us (2%)
  matrix products  2.29 us (1%)
  between operations  2.13 us (1%)
    all_to_all x2, blocking collectives, sent_to_all(): lax.all_to_all(jnp.broadcast_to(array[None], (devices, *array.shape)), ax...  43.1 us
    all_to_all x2, blocking collectives, sum_at_owner(): lax.all_to_all(cut_along(array, dim, devices), axis, 0, 0, tiled=True)  41.3 us
    all_to_all x1, waiting for transfers between devices, sum_at_owner(): lax.all_to_all(cut_along(array, dim, devices), axis, 0, 0, tiled=True)  15 us
    all_to_all x1, waiting for transfers between devices, sent_to_all(): lax.all_to_all(jnp.broadcast_to(array[None], (devices, *array.shape)), ax...  14.5 us
    all_to_all x1, starting transfers between devices, sent_to_all(): lax.all_to_all(jnp.broadcast_to(array[None], (devices, *array.shape)), ax...  7.89 us
    ppermute x2, waiting for transfers between devices, shifted(): return lax.ppermute(block, axis, route)  7.15 us
    all_to_all x1, starting transfers between devices, sum_at_owner(): lax.all_to_all(cut_along(array, dim, devices), axis, 0, 0, tiled=True)  4.77 us
    ppermute x2, starting transfers between devices, shifted(): return lax.ppermute(block, axis, route)  4.57 us
  transfers between devices with their start and end apart: 4, of which 4 were waited for; matrix products, arithmetic and copies ran while one was open for 2% of the time, Pallas kernels for 0%

commit v1 on v0

v1 whole, which is shorter than its diff:
```python
import jax
import jax.numpy as jnp
from jax import lax
from jax.experimental import pallas as pl
from jax.experimental.pallas import tpu as pltpu
from jax.sharding import PartitionSpec as P

PW = 256
TILE = 128
HALF = 64
W = 2048
NZ = 8
SIDE = 4
CHIPS = SIDE * SIDE
TICKS = 3
LANES = 128
F32 = jnp.float32
BF16 = jnp.bfloat16
MESH = pl.DeviceIdType.MESH
RING = (0, 1, 3, 2)
HOPS = (1, 3, 2)
SPREAD = tuple((a, b) for a in range(SIDE) for b in range(SIDE) if (a, b) != (0, 0))


def kernel(
    right_side, entering, first_updates, diag_inverse, tile_blocks, targets, order, count,
    sol_out, upd_out,
    given, enter, first, weights, blocks, placed, base, other_base, products, own_products,
    code_own, code_sib, code_send, codes, sol_send, sol_recv, back_send, back_recv,
    block_send, block_recv, last_send, last_recv,
    load_sem, sib_send, sib_recv, base_send, base_recv, code_s1, code_r1, code_s2, code_r2,
    ring_s1, ring_r1, ring_s2, ring_r2, back_s, back_r, red_s, red_r,
):
    s = lax.axis_index("chain")
    row = lax.axis_index("rows")
    core = lax.rem(row, 2)
    chip = row // 2
    x = lax.rem(chip, SIDE)
    y = chip // SIDE
    p1 = x + core * (y - x)
    p2 = y + core * (x - y)
    stride1 = 1 + 3 * core
    stride2 = 4 - 3 * core
    up = lax.rem(s + 1, NZ)
    down = lax.rem(s + NZ - 1, NZ)
    sibling = (s, row + 1 - 2 * core)

    def chip_at(d1, d2):
        return lax.rem(p1 + d1, SIDE) * stride1 + lax.rem(p2 + d2, SIDE) * stride2

    def at(plane, d1, d2):
        return (plane, chip_at(d1, d2) * 2 + core)

    def send(src, dst, ssem, rsem, device):
        copy = pltpu.make_async_remote_copy(
            src_ref=src, dst_ref=dst, send_sem=ssem, recv_sem=rsem,
            device_id=device, device_id_type=MESH,
        )
        copy.start()
        return copy

    barrier = pltpu.get_barrier_semaphore()
    partners = [sibling] + [at(s, a, b) for a, b in SPREAD]
    partners += [at(up, d, 0) for d in range(SIDE)] + [at(down, (SIDE - d) % SIDE, 0) for d in range(SIDE)]
    partners += [(up, row + 1 - 2 * core), (down, row + 1 - 2 * core)]
    for device in partners:
        pl.semaphore_signal(barrier, inc=1, device_id=device, device_id_type=MESH)

    my_rows = pl.ds(pl.multiple_of(core * HALF, HALF), HALF)
    tile_rows = pl.ds(pl.multiple_of(core * TILE, TILE), TILE)
    diag_rows = pl.ds(pl.multiple_of(2 * TILE + core * HALF, HALF), HALF)
    loads = [
        pltpu.make_async_copy(right_side, given, load_sem.at[0]),
        pltpu.make_async_copy(entering, enter, load_sem.at[1]),
        pltpu.make_async_copy(first_updates, first, load_sem.at[2]),
        pltpu.make_async_copy(tile_blocks.at[0, 0], weights.at[tile_rows], load_sem.at[3]),
        pltpu.make_async_copy(diag_inverse.at[0], weights.at[diag_rows], load_sem.at[4]),
    ]
    for copy in loads:
        copy.start()

    live = jnp.int32(0)
    for k in range(order.shape[1]):
        hit = jnp.logical_and(order[0, k] == row, k < count[0])
        live = live + hit.astype(jnp.int32)
    code = targets[0, 0] + CHIPS * (1 - live)
    code_rows = lax.broadcasted_iota(jnp.int32, (8, LANES), 0)
    code_own[...] = jnp.where(code_rows == core, code, 0)

    for copy in loads[:3]:
        copy.wait()
    is_first = (s == 0).astype(F32)

    def head_part(tick, half):
        lanes = pl.ds(pl.multiple_of(tick * PW + half * LANES, LANES), LANES)
        value = given[:, lanes].astype(F32)
        if tick == 0:
            taken = enter[:, pl.ds(pl.multiple_of(half * LANES, LANES), LANES)]
        else:
            lanes = pl.ds(pl.multiple_of((tick - 1) * PW + half * LANES, LANES), LANES)
            taken = is_first * first[:, lanes]
        return (value - taken).astype(BF16)

    for tick in range(TICKS):
        other_base[tick] = head_part(tick, 1 - core)
        base[tick, chip, my_rows] = head_part(tick, core)

    pl.semaphore_wait(barrier, len(partners))

    pending = []
    sib_base = []
    for tick in range(TICKS):
        sib_base.append(send(
            other_base.at[tick], base.at[tick, chip, my_rows],
            sib_send.at[tick], sib_recv.at[tick], sibling,
        ))
        if tick == 0:
            sib_code = send(code_own, code_sib, sib_send.at[3], sib_recv.at[3], sibling)
    sib_tile = send(tile_blocks.at[0, 0], weights.at[tile_rows], sib_send.at[4], sib_recv.at[4], sibling)
    sib_diag = send(diag_inverse.at[0], weights.at[diag_rows], sib_send.at[5], sib_recv.at[5], sibling)
    pending += sib_base + [sib_code, sib_tile, sib_diag]

    def gather_base(tick):
        sib_base[tick].wait_recv()
        copies = []
        for n, (a, b) in enumerate(SPREAD):
            copies.append(send(
                base.at[tick, chip], base.at[tick, chip],
                base_send.at[tick, n], base_recv.at[tick, n], at(s, a, b),
            ))
        pending.extend(copies)
        return copies

    arriving = gather_base(0)

    sib_code.wait_recv()
    code_send[...] = code_own[...] + code_sib[...]
    code_copies = {}
    for d in RING:
        code_copies[d] = send(code_send, codes.at[0, d], code_s1.at[d], code_r1.at[d], at(up, d, 0))
    pending.extend(code_copies.values())
    loads[3].wait()
    loads[4].wait()
    sib_tile.wait_recv()
    sib_diag.wait_recv()
    for b in range(CHIPS):
        blocks[b] = weights[:, b * TILE:(b + 1) * TILE]
    code_moves = []
    for d in RING:
        code_copies[d].wait_recv()
        for e in HOPS:
            code_moves.append(send(codes.at[0, d], codes.at[e, d], code_s2.at[e, d], code_r2.at[e, d], at(s, 0, e)))
    pending.extend(code_moves)
    for copy in arriving:
        copy.wait_recv()

    def dot(a, b):
        return jnp.dot(a, b, preferred_element_type=F32)

    def base_rows(tick):
        return base[tick].reshape(W, LANES)

    def product_rows(tick, e):
        return products[tick, e].reshape(SIDE * 2 * TILE, LANES)

    def placed_part(rows, e):
        return placed[rows, e * 1024:(e + 1) * 1024]

    TOP = slice(0, 2 * TILE)
    LOW = slice(2 * TILE, 3 * TILE)

    def send_products(tick):
        copies = {}
        for d in RING:
            copies[d] = send(
                own_products.at[tick], products.at[tick, 0, d],
                ring_s1.at[tick, d], ring_r1.at[tick, d], at(up, d, 0),
            )
        pending.extend(copies.values())
        return copies

    def forward_products(tick, copies):
        moves = {}
        for d in RING:
            copies[d].wait_recv()
            for e in HOPS:
                moves[e, d] = send(
                    products.at[tick, 0, d], products.at[tick, e, d],
                    ring_s2.at[tick, e, d], ring_r2.at[tick, e, d], at(s, 0, e),
                )
        pending.extend(moves.values())
        return moves

    sib_sol = []

    def give_solution(tick, value):
        lanes = pl.ds(pl.multiple_of(tick * PW + core * LANES, LANES), LANES)
        sol_send[tick] = value
        sol_out[:, lanes] = sol_send[tick, my_rows]
        theirs = pl.ds(pl.multiple_of((1 - core) * HALF, HALF), HALF)
        sib_sol.append(send(
            sol_send.at[tick, theirs], sol_recv.at[tick],
            sib_send.at[6 + tick], sib_recv.at[6 + tick], sibling,
        ))
        pending.append(sib_sol[-1])

    def code_of(e, d, k):
        return jnp.max(codes[e, d, k:k + 1, :])

    back_copies = []

    def give_back(tick):
        total = jnp.zeros((TILE, LANES), F32)
        for e in range(SIDE):
            for d in range(SIDE):
                for k in range(2):
                    part = products[tick, e, d, k * TILE:(k + 1) * TILE].astype(F32)
                    total = total + (code_list[e, d, k] == chip).astype(F32) * part
        back_send[tick] = total
        for h in range(2):
            back_copies.append(send(
                back_send.at[tick, h * HALF:(h + 1) * HALF], back_recv.at[tick, core],
                back_s.at[tick, h], back_r.at[tick, core], (down, chip * 2 + h),
            ))

    own_products[0] = dot(weights[TOP], base_rows(0)).astype(BF16)
    ring = send_products(0)
    arriving = gather_base(1)
    give_solution(0, dot(weights[LOW], base_rows(0)))
    moves = forward_products(0, ring)
    for copy in code_moves:
        copy.wait_recv()
    not_first = (s > 0).astype(F32)
    code_list = {}
    for e in range(SIDE):
        for d in range(SIDE):
            for k in range(2):
                value = code_of(e, d, k)
                code_list[e, d, k] = value
                block = lax.rem(value, CHIPS)
                used = jnp.full((1, LANES), (value < CHIPS).astype(F32) * not_first).astype(BF16)
                at_col = ((e * SIDE + d) * 2 + k) * TILE
                placed[:, at_col:at_col + TILE] = blocks[block] * used

    for tick in range(1, TICKS):
        for copy in arriving:
            copy.wait_recv()
        acc = dot(weights[TOP], base_rows(tick))
        for e in (0,) + HOPS:
            if e:
                for d in RING:
                    moves[e, d].wait_recv()
            acc = acc - dot(placed_part(TOP, e), product_rows(tick - 1, e))
        if tick < TICKS - 1:
            own_products[tick] = acc.astype(BF16)
            ring = send_products(tick)
            arriving = gather_base(tick + 1)
        else:
            code_both = [jnp.max(code_send[k:k + 1, :]) for k in range(2)]
            first_part, second_part = acc[:TILE], acc[TILE:]

            def reduced(target):
                m0 = (code_both[0] == target).astype(F32)
                m1 = (code_both[1] == target).astype(F32)
                return (m0 * first_part + m1 * second_part).astype(BF16)

            reds = []
            for n, (a, b) in enumerate(SPREAD):
                block_send[n] = reduced(chip_at(a, b))
                reds.append(send(block_send.at[n], block_recv.at[n], red_s.at[n], red_r.at[n], at(s, a, b)))
            pending.extend(reds)
            block_recv[CHIPS - 1] = reduced(chip)
        low = dot(weights[LOW], base_rows(tick))
        for e in range(SIDE):
            low = low - dot(placed_part(LOW, e), product_rows(tick - 1, e))
        give_solution(tick, low)
        give_back(tick - 1)
        if tick < TICKS - 1:
            moves = forward_products(tick, ring)

    for copy in reds:
        copy.wait_recv()
    total = jnp.zeros((TILE, LANES), F32)
    for n in range(CHIPS):
        total = total + block_recv[n].astype(F32)
    last_send[...] = total
    mine = pl.ds(pl.multiple_of((TICKS - 1) * PW + core * LANES, LANES), LANES)
    upd_out[:, mine] = last_send[my_rows]
    theirs = pl.ds(pl.multiple_of((1 - core) * HALF, HALF), HALF)
    last = send(last_send.at[theirs], last_recv, sib_send.at[9], sib_recv.at[9], sibling)
    pending.append(last)
    for tick in range(TICKS):
        lanes = pl.ds(pl.multiple_of(tick * PW + (1 - core) * LANES, LANES), LANES)
        sib_sol[tick].wait_recv()
        sol_out[:, lanes] = sol_recv[tick]
    for tick in range(TICKS - 1):
        for k in range(2):
            pltpu.make_async_copy(back_recv.at[tick, k], back_recv.at[tick, k], back_r.at[tick, k]).wait()
            upd_out[:, tick * PW + k * LANES:tick * PW + (k + 1) * LANES] = back_recv[tick, k]
    last.wait_recv()
    other = pl.ds(pl.multiple_of((TICKS - 1) * PW + (1 - core) * LANES, LANES), LANES)
    upd_out[:, other] = last_recv[...]
    for copy in pending + back_copies:
        copy.wait_send()


def body(*arrays):
    right_side = arrays[0]
    rows, width = right_side.shape
    dma = pltpu.SemaphoreType.DMA
    any_spec = pl.BlockSpec(memory_space=pl.ANY)
    smem = pl.BlockSpec(memory_space=pltpu.SMEM)
    vmem = pl.BlockSpec(memory_space=pltpu.VMEM)
    out = jax.ShapeDtypeStruct((rows, width), F32)
    n = len(SPREAD)
    return pl.pallas_call(
        kernel,
        out_shape=(out, out),
        in_specs=[any_spec] * 5 + [smem] * 3,
        out_specs=(vmem, vmem),
        scratch_shapes=[
            pltpu.VMEM((rows, width), BF16),
            pltpu.VMEM((rows, PW), F32),
            pltpu.VMEM((rows, 2 * PW), F32),
            pltpu.VMEM((3 * TILE, W), BF16),
            pltpu.VMEM((CHIPS, 3 * TILE, LANES), BF16),
            pltpu.VMEM((3 * TILE, 2 * W), BF16),
            pltpu.VMEM((TICKS, CHIPS, TILE, LANES), BF16),
            pltpu.VMEM((TICKS, HALF, LANES), BF16),
            pltpu.VMEM((TICKS - 1, SIDE, SIDE, 2 * TILE, LANES), BF16),
            pltpu.VMEM((TICKS - 1, 2 * TILE, LANES), BF16),
            pltpu.VMEM((8, LANES), jnp.int32),
            pltpu.VMEM((8, LANES), jnp.int32),
            pltpu.VMEM((8, LANES), jnp.int32),
            pltpu.VMEM((SIDE, SIDE, 8, LANES), jnp.int32),
            pltpu.VMEM((TICKS, TILE, LANES), F32),
            pltpu.VMEM((TICKS, HALF, LANES), F32),
            pltpu.VMEM((TICKS - 1, TILE, LANES), F32),
            pltpu.VMEM((TICKS - 1, 2, HALF, LANES), F32),
            pltpu.VMEM((n, TILE, LANES), BF16),
            pltpu.VMEM((CHIPS, TILE, LANES), BF16),
            pltpu.VMEM((TILE, LANES), F32),
            pltpu.VMEM((HALF, LANES), F32),
            dma((5,)), dma((10,)), dma((10,)),
            dma((TICKS, n)), dma((TICKS, n)),
            dma((SIDE,)), dma((SIDE,)), dma((SIDE, SIDE)), dma((SIDE, SIDE)),
            dma((2, SIDE)), dma((2, SIDE)), dma((2, SIDE, SIDE)), dma((2, SIDE, SIDE)),
            dma((2, 2)), dma((2, 2)),
            dma((n,)), dma((n,)),
        ],
        compiler_params=pltpu.CompilerParams(collective_id=0, has_side_effects=True),
        name="chain_solve",
    )(*arrays)


def solution(mesh):
    placed = (
        P(("chain", "rows"), None),
        P(("chain", "rows"), None),
        P("rows", None),
        P("chain", "rows", None),
        P("chain", "rows", None, None),
        P("chain", "rows"),
        P("chain", None),
        P("chain"),
    )
    return jax.shard_map(
        body,
        mesh=mesh,
        in_specs=placed,
        out_specs=(P(("chain", "rows"), None), P(("chain", "rows"), None)),
        check_vma=False,
    )
```

time: 154 us -> 71.4 us (0.46)
  the two profiles are of different devices: /device:TPU:129 before, /device:TPU:1 now
where the time goes in v1:
time: 71.4 us; the launch traced here: 71.3 us
  Pallas kernels  67 us (94%)
  local copies, waits for them, and re-layouts  2.34 us (3%)
  between operations  1.94 us (3%)
    pallas_call x1, Pallas kernels, body(): pl.pallas_call(kernel, out_shape=(out, out), in_specs=[any_spec] * 5 + [s...  67 us
    unnamed x4, local copies, waits for them, and re-layouts  2.34 us

profile of v1, /device:TPU:1, one launch (start us, length us, event | category | flops | bytes accessed | tf_op | source)
XLA Modules:
  0.0 71.3 jit_solution(7685282420007829769)
XLA Ops:
  1.9 67.0 %chain_solve.1 = (f32[64,768]{1,0:T(8,128)}, f32[64,768]{1,0:T(8,128)}) custom-call(bf16[64,768]{1,0:T(8,128)(2,1)} %right_side.1, f32[64,256]{1,0:T(8,128)} %entering.1, f32[64,512]{1,0:T(8,128)} %first_updates.1, bf16[1,64,2048]{2,1,0:T(8,128)(2,1)} %diag_inverse.1, bf16[1,1,128,2048]{3,2,1,0:T(8,128)(2,1)} %tile_blocks.1, s32[1,1]{1,0:T(1,128)S(6)} %copy.12.targets, ...), custom_call_target="tpu_custom_call" | custom-call | tf_op jit(solution)/shard_map/chain_solve/pallas_call | solution.py:316
  68.9 0.0 copy-start
  69.0 1.7 %copy.14 = f32[64,768]{1,0:T(8,128)} copy(f32[64,768]{1,0:T(8,128)} %get-tuple-element.4) | data formatting | bytes 393216
  70.6 0.0 copy-done
  70.6 0.7 copy.15
Async XLA Ops:
  68.9 1.7 %copy-start = (f32[64,768]{1,0:T(8,128)S(1)}, f32[64,768]{1,0:T(8,128)}, u32[]{:S(2)}) copy-start(f32[64,768]{1,0:T(8,128)} %get-tuple-element.5) | copy-start | bytes 589828

commit v2 on v0

v2 whole, which is shorter than its diff:
```python
import jax
import jax.numpy as jnp
from jax import lax
from jax.experimental import pallas as pl
from jax.experimental.pallas import tpu as pltpu
from jax.sharding import PartitionSpec as P

PW = 256
TILE = 128
HALF = 64
W = 2048
NZ = 8
SIDE = 4
CHIPS = SIDE * SIDE
TICKS = 3
LANES = 128
F32 = jnp.float32
BF16 = jnp.bfloat16
MESH = pl.DeviceIdType.MESH
HOPS = (1, 3, 2)
RING = (0,) + HOPS
FAR_FIRST = tuple((a, b) for a in range(SIDE - 1, -1, -1) for b in range(SIDE - 1, -1, -1) if (a, b) != (0, 0))
NODES = tuple((f, e) for e in RING for f in range(SIDE))
ROOTS = ((0, 0), (1, 0), (3, 0), (2, 0))
EVENTS = tuple(((f, 0), tuple((f, e) for e in HOPS)) for f in RING)
CHUNK = 8


def slot(f, e):
    return NODES.index((f, e))


def kernel(
    right_side, entering, first_updates, diag_inverse, tile_blocks, targets_in, order_in, count_in,
    sol_out, upd_out,
    targets, order, count, code_table,
    given, enter, first, weights, blocks, placed, base, other_base, products, own_products, acc,
    code_own, code_sib, code_send, codes, sol_send, sol_recv, back_send, back_recv,
    block_send, block_recv,
    load_sem, sib_send, sib_recv, base_s, base_r, code_s, code_r,
    ring_s, ring_r, back_s, back_r, red_s, red_r,
):
    s = lax.axis_index("chain")
    row = lax.axis_index("rows")
    core = lax.rem(row, 2)
    chip = row // 2
    x = lax.rem(chip, SIDE)
    y = chip // SIDE
    p1 = x + core * (y - x)
    p2 = y + core * (x - y)
    stride1 = 1 + 3 * core
    stride2 = 4 - 3 * core
    up = lax.rem(s + 1, NZ)
    down = lax.rem(s + NZ - 1, NZ)
    sibling = (s, row + 1 - 2 * core)

    def chip_at(d1, d2):
        return lax.rem(p1 + d1 + SIDE, SIDE) * stride1 + lax.rem(p2 + d2 + SIDE, SIDE) * stride2

    def at(plane, d1, d2):
        return (plane, chip_at(d1, d2) * 2 + core)

    def across(plane, d1, d2):
        return (plane, chip_at(d1, d2) * 2 + 1 - core)

    def remote(src, dst, ssem, rsem, device):
        return pltpu.make_async_remote_copy(
            src_ref=src, dst_ref=dst, send_sem=ssem, recv_sem=rsem,
            device_id=device, device_id_type=MESH,
        )

    def drain(ref, sem):
        pltpu.make_async_copy(ref, ref, sem).wait()

    barrier = pltpu.get_barrier_semaphore()

    def greet(device):
        pl.semaphore_signal(barrier, inc=1, device_id=device, device_id_type=MESH)

    greet(sibling)
    for a, b in FAR_FIRST:
        greet(at(s, a, b))
        greet(across(s, a, b))
    in_plane = 1 + 2 * len(FAR_FIRST)
    z_moves = [(f, 0) for f, _ in ROOTS] + [(0, f) for f, _ in ROOTS if f]
    in_z = len(z_moves) + 1
    for a, b in z_moves:
        greet(at(up, a, b))
        greet(at(down, SIDE - a, SIDE - b))
    greet(across(up, 0, 0))
    greet(across(down, 0, 0))

    my_rows = pl.ds(pl.multiple_of(core * HALF, HALF), HALF)
    their_rows = pl.ds(pl.multiple_of((1 - core) * HALF, HALF), HALF)
    tile_rows = pl.ds(pl.multiple_of(core * TILE, TILE), TILE)
    diag_rows = pl.ds(pl.multiple_of(2 * TILE + core * HALF, HALF), HALF)
    loads = [
        pltpu.make_async_copy(right_side, given, load_sem.at[0]),
        pltpu.make_async_copy(entering, enter, load_sem.at[1]),
        pltpu.make_async_copy(first_updates, first, load_sem.at[2]),
        pltpu.make_async_copy(targets_in, targets, load_sem.at[3]),
        pltpu.make_async_copy(order_in, order, load_sem.at[4]),
        pltpu.make_async_copy(count_in, count, load_sem.at[5]),
        pltpu.make_async_copy(tile_blocks.at[0, 0], weights.at[tile_rows], load_sem.at[6]),
        pltpu.make_async_copy(diag_inverse.at[0], weights.at[diag_rows], load_sem.at[7]),
    ]
    for copy in loads:
        copy.start()
    for copy in loads[:3]:
        copy.wait()
    is_first = (s == 0).astype(F32)

    def head_part(tick, half):
        lanes = pl.ds(pl.multiple_of(tick * PW + half * LANES, LANES), LANES)
        value = given[:, lanes].astype(F32)
        if tick == 0:
            taken = enter[:, pl.ds(pl.multiple_of(half * LANES, LANES), LANES)]
        else:
            lanes = pl.ds(pl.multiple_of((tick - 1) * PW + half * LANES, LANES), LANES)
            taken = is_first * first[:, lanes]
        return (value - taken).astype(BF16)

    for tick in range(TICKS):
        other_base[tick] = head_part(tick, 1 - core)
        base[tick, chip, my_rows] = head_part(tick, core)

    for copy in loads[3:6]:
        copy.wait()
    live = jnp.int32(0)
    for k in range(order.shape[1]):
        hit = jnp.logical_and(order[0, k] == row, k < count[0])
        live = live + hit.astype(jnp.int32)
    code = targets[0, 0] + CHIPS * (1 - live)
    code_rows = lax.broadcasted_iota(jnp.int32, (8, LANES), 0)
    code_own[...] = jnp.where(code_rows == core, code, 0)

    pl.semaphore_wait(barrier, in_plane + 2 * in_z)

    def sib_base(tick):
        return remote(
            other_base.at[tick], base.at[tick, chip, my_rows],
            sib_send.at[0], sib_recv.at[tick], sibling,
        )

    def sib_code():
        return remote(code_own, code_sib, sib_send.at[1], sib_recv.at[3], sibling)

    def sib_tile():
        return remote(tile_blocks.at[0, 0], weights.at[tile_rows], sib_send.at[2], sib_recv.at[4], sibling)

    def sib_diag():
        return remote(diag_inverse.at[0], weights.at[diag_rows], sib_send.at[3], sib_recv.at[5], sibling)

    def base_half(rows, d1, d2):
        return remote(
            base.at[0, chip, rows], base.at[0, chip, rows],
            base_s, base_r.at[0, 0], at(s, d1, d2),
        )

    n_far = len(FAR_FIRST)
    sib_base(0).start()
    sib_code().start()
    for a, b in FAR_FIRST:
        base_half(my_rows, a, b).start()
    sib_base(0).wait_recv()
    for a, b in FAR_FIRST:
        base_half(their_rows, b, a).start()
    sib_base(1).start()
    sib_base(2).start()

    def code_root(f, e):
        return remote(code_send, codes.at[slot(f, e)], code_s, code_r.at[0], at(up, f, e))

    def code_edge(node, child):
        n, m = slot(*node), slot(*child)
        return remote(
            codes.at[n], codes.at[m], code_s, code_r.at[1],
            at(s, child[0] - node[0], child[1] - node[1]),
        )

    sib_code().wait_recv()
    code_send[...] = code_own[...] + code_sib[...]

    for f, e in ROOTS:
        code_root(f, e).start()

    sib_tile().start()
    sib_diag().start()

    def base_copy(tick, node, child):
        held = chip_at(-node[0], -node[1])
        return remote(
            base.at[tick, held], base.at[tick, held], base_s, base_r.at[tick, int(child[1] > 0)],
            at(s, child[0] - node[0], child[1] - node[1]),
        )

    def base_along(tick):
        sib_base(tick).wait_recv()
        for f in HOPS:
            base_copy(tick, (0, 0), (f, 0)).start()

    def base_over(tick):
        drain(base.at[tick, :SIDE - 1], base_r.at[tick, 0])
        for f in RING:
            for e in HOPS:
                base_copy(tick, (f, 0), (f, e)).start()

    def base_done(tick):
        drain(base.at[tick, :CHIPS - SIDE], base_r.at[tick, 1])

    base_along(1)
    for copy in loads[6:]:
        copy.wait()
    sib_tile().wait_recv()
    sib_diag().wait_recv()
    for b in range(CHIPS):
        blocks[b] = weights[:, b * TILE:(b + 1) * TILE]

    drain(codes.at[:SIDE], code_r.at[0])
    for node, children in EVENTS:
        for child in children:
            code_edge(node, child).start()

    drain(base.at[0, :n_far], base_r.at[0, 0])

    def dot(a, b):
        return jnp.dot(a, b, preferred_element_type=F32)

    def base_rows(tick):
        return base[tick].reshape(W, LANES)

    TOP = slice(0, 2 * TILE)
    LOW = slice(2 * TILE, 3 * TILE)
    def placed_dot(rows, tick, k, part):
        first_slot = part * CHUNK
        col = (k * CHIPS + first_slot) * TILE
        right = products[tick, k, first_slot:first_slot + CHUNK].reshape(CHUNK * TILE, LANES)
        return dot(placed[rows, col:col + CHUNK * TILE], right)

    def move(k, f, e):
        return (f, e) if k == 0 else (e, f)

    def root(tick, k, node):
        n = slot(*node)
        return remote(
            own_products.at[tick, k], products.at[tick, k, n],
            ring_s, ring_r.at[tick, k, n], at(up, *move(k, *node)),
        )

    def edge(tick, k, node, child):
        n, m = slot(*node), slot(*child)
        return remote(
            products.at[tick, k, n], products.at[tick, k, m],
            ring_s, ring_r.at[tick, k, m if m < SIDE else SIDE + m // CHUNK],
            at(s, *move(k, child[0] - node[0], child[1] - node[1])),
        )

    def parts_in(tick, k, part):
        drain(products.at[tick, k, max(part * CHUNK, SIDE):(part + 1) * CHUNK], ring_r.at[tick, k, SIDE + part])

    def pass_on(tick):
        for j, (node, children) in enumerate(EVENTS):
            for k in range(2):
                drain(products.at[tick, k, slot(*node)], ring_r.at[tick, k, slot(*node)])
                for child in children:
                    edge(tick, k, node, child).start()

    def take_products(tick):
        for part in range(2):
            for k in range(2):
                parts_in(tick, k, part)
                acc[...] = acc[...] - placed_dot(TOP, tick, k, part)

    def give_back(tick):
        total = jnp.zeros((TILE, LANES), F32)
        for k in range(2):
            for n in range(CHIPS):
                part = products[tick, k, n].astype(F32)
                total = total + (code_table[k * CHIPS + n] == chip).astype(F32) * part
        back_send[tick] = total
        for h in range(2):
            back(tick, h, core).start()

    def back(tick, h, k):
        return remote(
            back_send.at[tick, h * HALF:(h + 1) * HALF], back_recv.at[tick, k],
            back_s, back_r, (down, chip * 2 + h),
        )

    code_both = [jnp.max(code_send[k:k + 1, :]) for k in range(2)]

    def own_half(n, a, b):
        return remote(
            block_send.at[n, my_rows], block_recv.at[core * CHIPS + n],
            red_s, red_r, at(s, a, b),
        )

    def other_half(n, a, b):
        return remote(
            block_send.at[n, their_rows], block_recv.at[core * CHIPS + n],
            red_s, red_r, across(s, a, b),
        )

    def reduce_out(tick):
        def reduced(target):
            m0 = (code_both[0] == target).astype(F32)
            m1 = (code_both[1] == target).astype(F32)
            return (m0 * acc[:TILE] + m1 * acc[TILE:]).astype(BF16)

        for n, (a, b) in enumerate(FAR_FIRST):
            block_send[n] = reduced(chip_at(a, b))
            own_half(n, a, b).start()
        block_send[n_far] = reduced(chip)
        other_half(n_far, 0, 0).start()
        for b, a in FAR_FIRST:
            n = FAR_FIRST.index((a, b))
            other_half(n, a, b).start()
        block_recv[core * CHIPS + n_far] = block_send[n_far, my_rows]

    def reduce_in(tick):
        drain(block_recv.at[:2 * CHIPS - 1], red_r)
        for k in range(2):
            total = jnp.zeros((HALF, LANES), F32)
            for n in range(CHIPS):
                total = total + block_recv[k * CHIPS + n].astype(F32)
            upd_out[:, tick * PW + k * LANES:tick * PW + (k + 1) * LANES] = total

    def sib_sol(tick):
        return remote(
            sol_send.at[tick, their_rows], sol_recv.at[tick],
            sib_send.at[4], sib_recv.at[6], sibling,
        )

    inner = s > 0

    def read_codes():
        drain(codes.at[SIDE:], code_r.at[1])
        for k in range(2):
            for n, (f, e) in enumerate(NODES):
                value = jnp.max(codes[slot(*move(k, f, e)), k:k + 1, :])
                code_table[k * CHIPS + n] = value
                block = lax.rem(value, CHIPS)
                used = jnp.full((1, LANES), (value < CHIPS).astype(F32)).astype(BF16)
                col = (k * CHIPS + n) * TILE
                placed[:, col:col + TILE] = blocks[block] * used

    for tick in range(TICKS):
        if tick:
            base_done(tick)
        acc[...] = dot(weights[TOP], base_rows(tick))
        if tick:
            @pl.when(inner)
            def _():
                take_products(tick - 1)
        if tick < TICKS - 1:
            for k in range(2):
                own_products[tick, k] = acc[k * TILE:(k + 1) * TILE].astype(BF16)
            for node in ROOTS:
                for k in range(2):
                    root(tick, k, node).start()
            base_over(tick + 1)
            if tick + 2 < TICKS:
                base_along(tick + 2)
        else:
            reduce_out(tick)
        sol_send[tick] = dot(weights[LOW], base_rows(tick))
        if tick:
            @pl.when(inner)
            def _():
                for k in range(2):
                    for part in range(2):
                        sol_send[tick] = sol_send[tick] - placed_dot(LOW, tick - 1, k, part)
                give_back(tick - 1)
        lanes = pl.ds(pl.multiple_of(tick * PW + core * LANES, LANES), LANES)
        sol_out[:, lanes] = sol_send[tick, my_rows]
        sib_sol(tick).start()
        if tick < TICKS - 1:
            @pl.when(inner)
            def _():
                pass_on(tick)
        if tick == 0:
            read_codes()
        if tick == 1:
            @pl.when(s == 0)
            def _():
                pass_on(0)

    @pl.when(s == 0)
    def _():
        for tick in range(TICKS - 1):
            if tick:
                pass_on(tick)
            for k in range(2):
                for part in range(2):
                    parts_in(tick, k, part)
            give_back(tick)

    drain(back_recv, back_r)
    for tick in range(TICKS - 1):
        for k in range(2):
            upd_out[:, tick * PW + k * LANES:tick * PW + (k + 1) * LANES] = back_recv[tick, k]
    drain(sol_recv, sib_recv.at[6])
    for tick in range(TICKS):
        lanes = pl.ds(pl.multiple_of(tick * PW + (1 - core) * LANES, LANES), LANES)
        sol_out[:, lanes] = sol_recv[tick]
    reduce_in(TICKS - 1)
    drain(other_base, sib_send.at[0])
    drain(code_own, sib_send.at[1])
    drain(weights.at[:TILE], sib_send.at[2])
    drain(weights.at[:HALF], sib_send.at[3])
    drain(sol_recv, sib_send.at[4])
    drain(base.at[:, :n_far], base_s)
    drain(codes, code_s)
    drain(products, ring_s)
    drain(back_send, back_s)
    drain(block_recv.at[:2 * CHIPS - 1], red_s)


def body(*arrays):
    right_side = arrays[0]
    rows, width = right_side.shape
    dma = pltpu.SemaphoreType.DMA
    any_spec = pl.BlockSpec(memory_space=pl.ANY)
    hbm_spec = pl.BlockSpec(memory_space=pltpu.HBM)
    vmem = pl.BlockSpec(memory_space=pltpu.VMEM)
    out = jax.ShapeDtypeStruct((rows, width), F32)
    return pl.pallas_call(
        kernel,
        out_shape=(out, out),
        in_specs=[any_spec] * 5 + [hbm_spec] * 3,
        out_specs=(vmem, vmem),
        scratch_shapes=[
            pltpu.SMEM(arrays[5].shape, jnp.int32),
            pltpu.SMEM(arrays[6].shape, jnp.int32),
            pltpu.SMEM(arrays[7].shape, jnp.int32),
            pltpu.SMEM((2 * CHIPS,), jnp.int32),
            pltpu.VMEM((rows, width), BF16),
            pltpu.VMEM((rows, PW), F32),
            pltpu.VMEM((rows, 2 * PW), F32),
            pltpu.VMEM((3 * TILE, W), BF16),
            pltpu.VMEM((CHIPS, 3 * TILE, LANES), BF16),
            pltpu.VMEM((3 * TILE, 2 * W), BF16),
            pltpu.VMEM((TICKS, CHIPS, TILE, LANES), BF16),
            pltpu.VMEM((TICKS, HALF, LANES), BF16),
            pltpu.VMEM((TICKS - 1, 2, CHIPS, TILE, LANES), BF16),
            pltpu.VMEM((TICKS - 1, 2, TILE, LANES), BF16),
            pltpu.VMEM((2 * TILE, LANES), F32),
            pltpu.VMEM((8, LANES), jnp.int32),
            pltpu.VMEM((8, LANES), jnp.int32),
            pltpu.VMEM((8, LANES), jnp.int32),
            pltpu.VMEM((CHIPS, 8, LANES), jnp.int32),
            pltpu.VMEM((TICKS, TILE, LANES), F32),
            pltpu.VMEM((TICKS, HALF, LANES), F32),
            pltpu.VMEM((TICKS - 1, TILE, LANES), F32),
            pltpu.VMEM((TICKS - 1, 2, HALF, LANES), F32),
            pltpu.VMEM((CHIPS, TILE, LANES), BF16),
            pltpu.VMEM((2 * CHIPS, HALF, LANES), BF16),
            dma((8,)), dma((5,)), dma((7,)),
            dma, dma((TICKS, 2)), dma, dma((2,)),
            dma, dma((2, 2, SIDE + 2)), dma, dma, dma, dma,
        ],
        compiler_params=pltpu.CompilerParams(collective_id=0, has_side_effects=True),
        name="chain_solve",
    )(*arrays)


def solution(mesh):
    placed = (
        P(("chain", "rows"), None),
        P(("chain", "rows"), None),
        P("rows", None),
        P("chain", "rows", None),
        P("chain", "rows", None, None),
        P("chain", "rows"),
        P("chain", None),
        P("chain"),
    )
    return jax.shard_map(
        body,
        mesh=mesh,
        in_specs=placed,
        out_specs=(P(("chain", "rows"), None), P(("chain", "rows"), None)),
        check_vma=False,
    )
```

time: 154 us -> 58.7 us (0.38)
  the two profiles are of different devices: /device:TPU:129 before, /device:TPU:4 now
where the time goes in v2:
time: 58.7 us; the launch traced here: 58.5 us
  Pallas kernels  54.2 us (92%)
  local copies, waits for them, and re-layouts  2.34 us (4%)
  between operations  1.94 us (3%)
    pallas_call x1, Pallas kernels, body(): pl.pallas_call(kernel, out_shape=(out, out), in_specs=[any_spec] * 5 + [h...  54.2 us
    unnamed x4, local copies, waits for them, and re-layouts  2.34 us

profile of v2, /device:TPU:4, one launch (start us, length us, event | category | flops | bytes accessed | tf_op | source)
XLA Modules:
  0.0 58.5 jit_solution(3790569006526179527)
XLA Ops:
  1.9 54.2 %chain_solve.1 = (f32[64,768]{1,0:T(8,128)}, f32[64,768]{1,0:T(8,128)}) custom-call(bf16[64,768]{1,0:T(8,128)(2,1)} %right_side.1, f32[64,256]{1,0:T(8,128)} %entering.1, f32[64,512]{1,0:T(8,128)} %first_updates.1, bf16[1,64,2048]{2,1,0:T(8,128)(2,1)} %diag_inverse.1, bf16[1,1,128,2048]{3,2,1,0:T(8,128)(2,1)} %tile_blocks.1, s32[1,1]{1,0:T(1,128)S(6)} %copy.12.targets_in, ...), custom_call_target="tpu_custom_call" | custom-call | tf_op jit(solution)/shard_map/chain_solve/pallas_call | solution.py:427
  56.2 0.0 copy-start
  56.2 1.7 %copy.14 = f32[64,768]{1,0:T(8,128)} copy(f32[64,768]{1,0:T(8,128)} %get-tuple-element.4) | data formatting | bytes 393216
  57.8 0.0 copy-done
  57.8 0.7 %copy.15 = f32[64,768]{1,0:T(8,128)} copy(f32[64,768]{1,0:T(8,128)S(1)} %copy-done) | data formatting | bytes 393216
Async XLA Ops:
  56.2 1.7 %copy-start = (f32[64,768]{1,0:T(8,128)S(1)}, f32[64,768]{1,0:T(8,128)}, u32[]{:S(2)}) copy-start(f32[64,768]{1,0:T(8,128)} %get-tuple-element.5) | copy-start | bytes 589828

commit v3 on v2

--- a/solution.py
+++ b/solution.py
@@ -38,7 +38,7 @@
     code_own, code_sib, code_send, codes, sol_send, sol_recv, back_send, back_recv,
     block_send, block_recv,
     load_sem, sib_send, sib_recv, base_s, base_r, code_s, code_r,
-    ring_s, ring_r, back_s, back_r, red_s, red_r,
+    ring_s, ring_r, back_s, back_r, red_s, red_r, last_in,
 ):
     s = lax.axis_index("chain")
     row = lax.axis_index("rows")
@@ -85,10 +85,14 @@
     z_moves = [(f, 0) for f, _ in ROOTS] + [(0, f) for f, _ in ROOTS if f]
     in_z = len(z_moves) + 1
     for a, b in z_moves:
-        greet(at(up, a, b))
         greet(at(down, SIDE - a, SIDE - b))
-    greet(across(up, 0, 0))
     greet(across(down, 0, 0))
+
+    @pl.when(s < NZ - 1)
+    def _():
+        for a, b in z_moves:
+            greet(at(up, a, b))
+        greet(across(up, 0, 0))
 
     my_rows = pl.ds(pl.multiple_of(core * HALF, HALF), HALF)
     their_rows = pl.ds(pl.multiple_of((1 - core) * HALF, HALF), HALF)
@@ -134,7 +138,12 @@
     code_rows = lax.broadcasted_iota(jnp.int32, (8, LANES), 0)
     code_own[...] = jnp.where(code_rows == core, code, 0)
 
-    pl.semaphore_wait(barrier, in_plane + 2 * in_z)
+    pl.semaphore_wait(barrier, in_plane + in_z + in_z * (s > 0).astype(jnp.int32))
+
+    @pl.when(s == NZ - 1)
+    def _():
+        for device in (at(up, 0, 0), across(up, 0, 0)):
+            pl.semaphore_signal(last_in, inc=1, device_id=device, device_id_type=MESH)
 
     def sib_base(tick):
         return remote(
@@ -199,9 +208,10 @@
         for f in HOPS:
             base_copy(tick, (0, 0), (f, 0)).start()
 
-    def base_over(tick):
-        drain(base.at[tick, :SIDE - 1], base_r.at[tick, 0])
-        for f in RING:
+    def base_over(tick, rings=RING):
+        if rings[0] == 0:
+            drain(base.at[tick, :SIDE - 1], base_r.at[tick, 0])
+        for f in rings:
             for e in HOPS:
                 base_copy(tick, (f, 0), (f, e)).start()
 
@@ -209,6 +219,7 @@
         drain(base.at[tick, :CHIPS - SIDE], base_r.at[tick, 1])
 
     base_along(1)
+    base_along(2)
     for copy in loads[6:]:
         copy.wait()
     sib_tile().wait_recv()
@@ -216,11 +227,18 @@
     for b in range(CHIPS):
         blocks[b] = weights[:, b * TILE:(b + 1) * TILE]
 
-    drain(codes.at[:SIDE], code_r.at[0])
-    for node, children in EVENTS:
-        for child in children:
-            code_edge(node, child).start()
-
+    def pass_codes():
+        drain(codes.at[:SIDE], code_r.at[0])
+        for node, children in EVENTS:
+            for child in children:
+                code_edge(node, child).start()
+
+    @pl.when(s > 0)
+    def _():
+        pass_codes()
+
+
+    base_over(1, RING)
     drain(base.at[0, :n_far], base_r.at[0, 0])
 
     def dot(a, b):
@@ -333,16 +351,17 @@
 
     inner = s > 0
 
-    def read_codes():
+    def read_codes(place):
         drain(codes.at[SIDE:], code_r.at[1])
         for k in range(2):
             for n, (f, e) in enumerate(NODES):
                 value = jnp.max(codes[slot(*move(k, f, e)), k:k + 1, :])
                 code_table[k * CHIPS + n] = value
-                block = lax.rem(value, CHIPS)
-                used = jnp.full((1, LANES), (value < CHIPS).astype(F32)).astype(BF16)
-                col = (k * CHIPS + n) * TILE
-                placed[:, col:col + TILE] = blocks[block] * used
+                if place:
+                    block = lax.rem(value, CHIPS)
+                    used = jnp.full((1, LANES), (value < CHIPS).astype(F32)).astype(BF16)
+                    col = (k * CHIPS + n) * TILE
+                    placed[:, col:col + TILE] = blocks[block] * used
 
     for tick in range(TICKS):
         if tick:
@@ -358,9 +377,6 @@
             for node in ROOTS:
                 for k in range(2):
                     root(tick, k, node).start()
-            base_over(tick + 1)
-            if tick + 2 < TICKS:
-                base_along(tick + 2)
         else:
             reduce_out(tick)
         sol_send[tick] = dot(weights[LOW], base_rows(tick))
@@ -379,14 +395,21 @@
             def _():
                 pass_on(tick)
         if tick == 0:
-            read_codes()
+            base_over(2, RING)
+        if tick == 0:
+            @pl.when(inner)
+            def _():
+                read_codes(True)
         if tick == 1:
             @pl.when(s == 0)
             def _():
+                pass_codes()
                 pass_on(0)
 
     @pl.when(s == 0)
     def _():
+        read_codes(False)
+        pl.semaphore_wait(last_in, 2)
         for tick in range(TICKS - 1):
             if tick:
                 pass_on(tick)
@@ -423,7 +446,7 @@
     any_spec = pl.BlockSpec(memory_space=pl.ANY)
     hbm_spec = pl.BlockSpec(memory_space=pltpu.HBM)
     vmem = pl.BlockSpec(memory_space=pltpu.VMEM)
-    out = jax.ShapeDtypeStruct((rows, width), F32)
+    out = pltpu.VMEM((rows, width), F32)
     return pl.pallas_call(
         kernel,
         out_shape=(out, out),
@@ -458,6 +481,7 @@
             dma((8,)), dma((5,)), dma((7,)),
             dma, dma((TICKS, 2)), dma, dma((2,)),
             dma, dma((2, 2, SIDE + 2)), dma, dma, dma, dma,
+            pltpu.SemaphoreType.REGULAR,
         ],
         compiler_params=pltpu.CompilerParams(collective_id=0, has_side_effects=True),
         name="chain_solve",

time: 58.7 us -> 54.1 us (0.922)
  the two profiles are of different devices: /device:TPU:4 before, /device:TPU:129 now
where the time goes in v3:
time: 54.1 us; the launch traced here: 54 us
  Pallas kernels  50.7 us (94%)
  between operations  1.93 us (4%)
  local copies, waits for them, and re-layouts  1.36 us (3%)
    pallas_call x1, Pallas kernels, body(): pl.pallas_call(kernel, out_shape=(out, out), in_specs=[any_spec] * 5 + [h...  50.7 us
    unnamed x2, local copies, waits for them, and re-layouts  1.36 us

profile of v3, /device:TPU:129, one launch (start us, length us, event | category | flops | bytes accessed | tf_op | source)
XLA Modules:
  0.0 54.0 jit_solution(3624511914460755639)
XLA Ops:
  1.9 50.7 %chain_solve.1 = (f32[64,768]{1,0:T(8,128)S(1)}, f32[64,768]{1,0:T(8,128)S(1)}) custom-call(bf16[64,768]{1,0:T(8,128)(2,1)} %right_side.1, f32[64,256]{1,0:T(8,128)} %entering.1, f32[64,512]{1,0:T(8,128)} %first_updates.1, bf16[1,64,2048]{2,1,0:T(8,128)(2,1)} %diag_inverse.1, bf16[1,1,128,2048]{3,2,1,0:T(8,128)(2,1)} %tile_blocks.1, ...), custom_call_target="tpu_custom_call" | custom-call | tf_op jit(solution)/shard_map/chain_solve/pallas_call | solution.py:450
  52.6 0.7 %copy.12 = f32[64,768]{1,0:T(8,128)} copy(f32[64,768]{1,0:T(8,128)S(1)} %get-tuple-element.2) | data formatting | bytes 393216
  53.3 0.7 %copy.13 = f32[64,768]{1,0:T(8,128)} copy(f32[64,768]{1,0:T(8,128)S(1)} %get-tuple-element.3) | data formatting | bytes 393216

commit v4 on v3

--- a/solution.py
+++ b/solution.py
@@ -167,35 +167,6 @@
         )
 
     n_far = len(FAR_FIRST)
-    sib_base(0).start()
-    sib_code().start()
-    for a, b in FAR_FIRST:
-        base_half(my_rows, a, b).start()
-    sib_base(0).wait_recv()
-    for a, b in FAR_FIRST:
-        base_half(their_rows, b, a).start()
-    sib_base(1).start()
-    sib_base(2).start()
-
-    def code_root(f, e):
-        return remote(code_send, codes.at[slot(f, e)], code_s, code_r.at[0], at(up, f, e))
-
-    def code_edge(node, child):
-        n, m = slot(*node), slot(*child)
-        return remote(
-            codes.at[n], codes.at[m], code_s, code_r.at[1],
-            at(s, child[0] - node[0], child[1] - node[1]),
-        )
-
-    sib_code().wait_recv()
-    code_send[...] = code_own[...] + code_sib[...]
-
-    for f, e in ROOTS:
-        code_root(f, e).start()
-
-    sib_tile().start()
-    sib_diag().start()
-
     def base_copy(tick, node, child):
         held = chip_at(-node[0], -node[1])
         return remote(
@@ -218,7 +189,38 @@
     def base_done(tick):
         drain(base.at[tick, :CHIPS - SIDE], base_r.at[tick, 1])
 
-    base_along(1)
+    sib_base(0).start()
+    sib_base(1).start()
+    sib_code().start()
+    for a, b in FAR_FIRST:
+        base_half(my_rows, a, b).start()
+    sib_base(0).wait_recv()
+    sib_base(1).wait_recv()
+    for f in HOPS:
+        base_copy(1, (0, 0), (f, 0)).start()
+    for a, b in FAR_FIRST:
+        base_half(their_rows, b, a).start()
+    sib_base(2).start()
+
+    def code_root(f, e):
+        return remote(code_send, codes.at[slot(f, e)], code_s, code_r.at[0], at(up, f, e))
+
+    def code_edge(node, child):
+        n, m = slot(*node), slot(*child)
+        return remote(
+            codes.at[n], codes.at[m], code_s, code_r.at[1],
+            at(s, child[0] - node[0], child[1] - node[1]),
+        )
+
+    sib_code().wait_recv()
+    code_send[...] = code_own[...] + code_sib[...]
+
+    for f, e in ROOTS:
+        code_root(f, e).start()
+
+    sib_tile().start()
+    sib_diag().start()
+
     base_along(2)
     for copy in loads[6:]:
         copy.wait()
@@ -232,10 +234,6 @@
         for node, children in EVENTS:
             for child in children:
                 code_edge(node, child).start()
-
-    @pl.when(s > 0)
-    def _():
-        pass_codes()
 
 
     base_over(1, RING)
@@ -371,6 +369,11 @@
             @pl.when(inner)
             def _():
                 take_products(tick - 1)
+        if tick == 1:
+            @pl.when(s == 0)
+            def _():
+                pass_codes()
+                pass_on(0)
         if tick < TICKS - 1:
             for k in range(2):
                 own_products[tick, k] = acc[k * TILE:(k + 1) * TILE].astype(BF16)
@@ -379,6 +382,10 @@
                     root(tick, k, node).start()
         else:
             reduce_out(tick)
+        if tick == 0:
+            @pl.when(inner)
+            def _():
+                pass_codes()
         sol_send[tick] = dot(weights[LOW], base_rows(tick))
         if tick:
             @pl.when(inner)
@@ -400,11 +407,6 @@
             @pl.when(inner)
             def _():
                 read_codes(True)
-        if tick == 1:
-            @pl.when(s == 0)
-            def _():
-                pass_codes()
-                pass_on(0)
 
     @pl.when(s == 0)
     def _():

time: 54.1 us -> 51.9 us (0.959)
  Pallas kernels: 50.7 us -> 48.5 us
    pallas_call x1, Pallas kernels: 50.7 us -> 48.5 us  [body(): pl.pallas_call(kernel, out_shape=(out, out), in_specs=[any_spec] * 5 + [h...]
where the time goes in v4:
time: 51.9 us; the launch traced here: 51.8 us
  Pallas kernels  48.5 us (93%)
  between operations  1.93 us (4%)
  local copies, waits for them, and re-layouts  1.36 us (3%)
    pallas_call x1, Pallas kernels, body(): pl.pallas_call(kernel, out_shape=(out, out), in_specs=[any_spec] * 5 + [h...  48.5 us
    unnamed x2, local copies, waits for them, and re-layouts  1.36 us

profile of v4, /device:TPU:129, one launch (start us, length us, event | category | flops | bytes accessed | tf_op | source)
XLA Modules:
  0.0 51.8 jit_solution(15560782628376862070)
XLA Ops:
  1.9 48.5 %chain_solve.1 = (f32[64,768]{1,0:T(8,128)S(1)}, f32[64,768]{1,0:T(8,128)S(1)}) custom-call(bf16[64,768]{1,0:T(8,128)(2,1)} %right_side.1, f32[64,256]{1,0:T(8,128)} %entering.1, f32[64,512]{1,0:T(8,128)} %first_updates.1, bf16[1,64,2048]{2,1,0:T(8,128)(2,1)} %diag_inverse.1, bf16[1,1,128,2048]{3,2,1,0:T(8,128)(2,1)} %tile_blocks.1, ...), custom_call_target="tpu_custom_call" | custom-call | tf_op jit(solution)/shard_map/chain_solve/pallas_call | solution.py:452
  50.4 0.7 %copy.12 = f32[64,768]{1,0:T(8,128)} copy(f32[64,768]{1,0:T(8,128)S(1)} %get-tuple-element.2) | data formatting | bytes 393216
  51.1 0.7 %copy.13 = f32[64,768]{1,0:T(8,128)} copy(f32[64,768]{1,0:T(8,128)S(1)} %get-tuple-element.3) | data formatting | bytes 393216

commit v5 on v4

--- a/solution.py
+++ b/solution.py
@@ -32,7 +32,7 @@
 
 def kernel(
     right_side, entering, first_updates, diag_inverse, tile_blocks, targets_in, order_in, count_in,
-    sol_out, upd_out,
+    both_out,
     targets, order, count, code_table,
     given, enter, first, weights, blocks, placed, base, other_base, products, own_products, acc,
     code_own, code_sib, code_send, codes, sol_send, sol_recv, back_send, back_recv,
@@ -40,6 +40,8 @@
     load_sem, sib_send, sib_recv, base_s, base_r, code_s, code_r,
     ring_s, ring_r, back_s, back_r, red_s, red_r, last_in,
 ):
+    rows_out = both_out.shape[0] // 2
+    sol_out, upd_out = both_out.at[:rows_out], both_out.at[rows_out:]
     s = lax.axis_index("chain")
     row = lax.axis_index("rows")
     core = lax.rem(row, 2)
@@ -448,12 +450,12 @@
     any_spec = pl.BlockSpec(memory_space=pl.ANY)
     hbm_spec = pl.BlockSpec(memory_space=pltpu.HBM)
     vmem = pl.BlockSpec(memory_space=pltpu.VMEM)
-    out = pltpu.VMEM((rows, width), F32)
-    return pl.pallas_call(
+    out = pltpu.VMEM((2 * rows, width), F32)
+    both = pl.pallas_call(
         kernel,
-        out_shape=(out, out),
+        out_shape=out,
         in_specs=[any_spec] * 5 + [hbm_spec] * 3,
-        out_specs=(vmem, vmem),
+        out_specs=vmem,
         scratch_shapes=[
             pltpu.SMEM(arrays[5].shape, jnp.int32),
             pltpu.SMEM(arrays[6].shape, jnp.int32),
@@ -488,6 +490,7 @@
         compiler_params=pltpu.CompilerParams(collective_id=0, has_side_effects=True),
         name="chain_solve",
     )(*arrays)
+    return both[:rows], both[rows:]
 
 
 def solution(mesh):

time: 51.9 us -> 51.3 us (0.988)
  local copies, waits for them, and re-layouts: 1.36 us -> 0.77 us
    unnamed x2 -> x0, local copies, waits for them, and re-layouts: 1.36 us -> none
    slice x0 -> x1, local copies, waits for them, and re-layouts: none -> 0.77 us  [body(): return (both[:rows], both[rows:])]
where the time goes in v5:
time: 51.3 us; the launch traced here: 51.2 us
  Pallas kernels  48.5 us (95%)
  between operations  1.93 us (4%)
  local copies, waits for them, and re-layouts  0.77 us (2%)
    pallas_call x1, Pallas kernels, body(): pl.pallas_call(kernel, out_shape=out, in_specs=[any_spec] * 5 + [hbm_spec...  48.5 us

profile of v5, /device:TPU:129, one launch (start us, length us, event | category | flops | bytes accessed | tf_op | source)
XLA Modules:
  0.0 51.2 jit_solution(5900330173398986980)
XLA Ops:
  1.9 48.5 %chain_solve.1 = f32[128,768]{1,0:T(8,128)S(1)} custom-call(bf16[64,768]{1,0:T(8,128)(2,1)} %right_side.1, f32[64,256]{1,0:T(8,128)} %entering.1, f32[64,512]{1,0:T(8,128)} %first_updates.1, bf16[1,64,2048]{2,1,0:T(8,128)(2,1)} %diag_inverse.1, bf16[1,1,128,2048]{3,2,1,0:T(8,128)(2,1)} %tile_blocks.1, s32[1,1]{1,0:T(1,128)S(6)} %copy.10.targets_in, ...), custom_call_target="tpu_custom_call" | custom-call | tf_op jit(solution)/shard_map/chain_solve/pallas_call | solution.py:454
  50.4 0.8 %fusion = (f32[64,768]{1,0:T(8,128)}, f32[64,768]{1,0:T(8,128)}) fusion(f32[128,768]{1,0:T(8,128)S(1)} %chain_solve.1), kind=kLoop, calls=%fused_computation | loop fusion | bytes 786432 | tf_op jit(solution)/shard_map/slice | solution.py:493

commit v6 on v5

--- a/solution.py
+++ b/solution.py
@@ -227,9 +227,6 @@
     for copy in loads[6:]:
         copy.wait()
     sib_tile().wait_recv()
-    sib_diag().wait_recv()
-    for b in range(CHIPS):
-        blocks[b] = weights[:, b * TILE:(b + 1) * TILE]
 
     def pass_codes():
         drain(codes.at[:SIDE], code_r.at[0])
@@ -280,7 +277,7 @@
         for j, (node, children) in enumerate(EVENTS):
             for k in range(2):
                 drain(products.at[tick, k, slot(*node)], ring_r.at[tick, k, slot(*node)])
-                for child in children:
+                for child in (children if k == 0 else children[1::-1] + children[2:]):
                     edge(tick, k, node, child).start()
 
     def take_products(tick):
@@ -388,6 +385,10 @@
             @pl.when(inner)
             def _():
                 pass_codes()
+        if tick == 0:
+            sib_diag().wait_recv()
+            for b in range(CHIPS):
+                blocks[b] = weights[:, b * TILE:(b + 1) * TILE]
         sol_send[tick] = dot(weights[LOW], base_rows(tick))
         if tick:
             @pl.when(inner)

time: 51.3 us -> 51.3 us (level)
  no operation moved by 1% of the time
where the time goes in v6:
time: 51.3 us; the launch traced here: 51.2 us
  Pallas kernels  48.5 us (95%)
  between operations  1.93 us (4%)
  local copies, waits for them, and re-layouts  0.77 us (2%)
    pallas_call x1, Pallas kernels, body(): pl.pallas_call(kernel, out_shape=out, in_specs=[any_spec] * 5 + [hbm_spec...  48.5 us

profile of v6, /device:TPU:129, one launch (start us, length us, event | category | flops | bytes accessed | tf_op | source)
XLA Modules:
  0.0 51.2 jit_solution(16168931624365920507)
XLA Ops:
  1.9 48.5 %chain_solve.1 = f32[128,768]{1,0:T(8,128)S(1)} custom-call(bf16[64,768]{1,0:T(8,128)(2,1)} %right_side.1, f32[64,256]{1,0:T(8,128)} %entering.1, f32[64,512]{1,0:T(8,128)} %first_updates.1, bf16[1,64,2048]{2,1,0:T(8,128)(2,1)} %diag_inverse.1, bf16[1,1,128,2048]{3,2,1,0:T(8,128)(2,1)} %tile_blocks.1, s32[1,1]{1,0:T(1,128)S(6)} %copy.10.targets_in, ...), custom_call_target="tpu_custom_call" | custom-call | tf_op jit(solution)/shard_map/chain_solve/pallas_call | solution.py:455
  50.4 0.8 %fusion = (f32[64,768]{1,0:T(8,128)}, f32[64,768]{1,0:T(8,128)}) fusion(f32[128,768]{1,0:T(8,128)S(1)} %chain_solve.1), kind=kLoop, calls=%fused_computation | loop fusion | bytes 786432 | tf_op jit(solution)/shard_map/slice | solution.py:494

commit v7 on v5

--- a/solution.py
+++ b/solution.py
@@ -178,14 +178,14 @@
 
     def base_along(tick):
         sib_base(tick).wait_recv()
-        for f in HOPS:
+        for f in (3, 1, 2):
             base_copy(tick, (0, 0), (f, 0)).start()
 
     def base_over(tick, rings=RING):
         if rings[0] == 0:
             drain(base.at[tick, :SIDE - 1], base_r.at[tick, 0])
         for f in rings:
-            for e in HOPS:
+            for e in (3, 1, 2):
                 base_copy(tick, (f, 0), (f, e)).start()
 
     def base_done(tick):

time: 51.3 us -> 51.3 us (level)
  no operation moved by 1% of the time
where the time goes in v7:
time: 51.3 us; the launch traced here: 51.2 us
  Pallas kernels  48.5 us (95%)
  between operations  1.93 us (4%)
  local copies, waits for them, and re-layouts  0.77 us (2%)
    pallas_call x1, Pallas kernels, body(): pl.pallas_call(kernel, out_shape=out, in_specs=[any_spec] * 5 + [hbm_spec...  48.5 us

profile of v7, /device:TPU:129, one launch (start us, length us, event | category | flops | bytes accessed | tf_op | source)
XLA Modules:
  0.0 51.2 jit_solution(17261109799355671602)
XLA Ops:
  1.9 48.5 %chain_solve.1 = f32[128,768]{1,0:T(8,128)S(1)} custom-call(bf16[64,768]{1,0:T(8,128)(2,1)} %right_side.1, f32[64,256]{1,0:T(8,128)} %entering.1, f32[64,512]{1,0:T(8,128)} %first_updates.1, bf16[1,64,2048]{2,1,0:T(8,128)(2,1)} %diag_inverse.1, bf16[1,1,128,2048]{3,2,1,0:T(8,128)(2,1)} %tile_blocks.1, s32[1,1]{1,0:T(1,128)S(6)} %copy.10.targets_in, ...), custom_call_target="tpu_custom_call" | custom-call | tf_op jit(solution)/shard_map/chain_solve/pallas_call | solution.py:454
  50.4 0.8 %fusion = (f32[64,768]{1,0:T(8,128)}, f32[64,768]{1,0:T(8,128)}) fusion(f32[128,768]{1,0:T(8,128)S(1)} %chain_solve.1), kind=kLoop, calls=%fused_computation | loop fusion | bytes 786432 | tf_op jit(solution)/shard_map/slice | solution.py:493
